TPU v7x, 32 devices: a whole 2x2x4 slice. The times are simulated.
32 devices in a mesh: dp: 16 (over z, y, core), mp: 2 (over x).
Axes of the slice: x: 2, y: 2, z: 4, core: 2. Of those that a mesh axis runs over, the one named last changes fastest.
Arguments:
- features: bfloat16 [2048, 4608], P('dp'), may hold values from -6 to 6
- proj_in: bfloat16 [4608, 2560], P('dp', 'mp'), may hold values from -0.09375 to 0.09375
- proj_out: bfloat16 [2560, 2560], P('mp'), may hold values from -0.125 to 0.125
- expert_gate: bfloat16 [64, 2560, 1536], P('dp', None, 'mp'), may hold values from -0.125 to 0.125
- expert_up: bfloat16 [64, 2560, 1536], P('dp', None, 'mp'), may hold values from -0.125 to 0.125
- expert_down: bfloat16 [64, 1536, 2560], P('dp', 'mp'), may hold values from -0.15625 to 0.15625
- routes: int32 [2048, 6], P('dp'), may hold values from 0 to 63, all different within a row; in each aligned block of 128 rows (0 to 127, 128 to 255, ...) at most 15 rows name the same one
- gate_weights: float32 [2048, 6], P('dp'), may hold values from 0.1 to 0.6
- cotangent: bfloat16 [2048, 2560], P('dp'), may hold values from -0.09375 to 0.09375
- first_in: float32 [4608, 2560], P('dp', 'mp'), may hold values from -2 to 2
- second_in: float32 [4608, 2560], P('dp', 'mp'), may hold values from 0.02 to 1
- first_out: float32 [2560, 2560], P('mp', 'dp'), may hold values from -2 to 2
- second_out: float32 [2560, 2560], P('mp', 'dp'), may hold values from 0.02 to 1
Outputs:
- moe_out: bfloat16 [2048, 2560], P('dp')
- new_proj_in: bfloat16 [4608, 2560], P('dp', 'mp')
- new_proj_out: bfloat16 [2560, 2560], P('mp', 'dp')
- new_first_in: float32 [4608, 2560], P('dp', 'mp')
- new_second_in: float32 [4608, 2560], P('dp', 'mp')
- new_first_out: float32 [2560, 2560], P('mp', 'dp')
- new_second_out: float32 [2560, 2560], P('mp', 'dp')
Inputs may be any that keep to these rules, and one draw needn't show every extreme that they name: `routes`: each row names 6 different experts. Within the rows of one device (aligned blocks of 128 rows) no expert is named more than 15 times, and in every draw some expert is named exactly 15 times in some block.
All inputs are finite; a program needn't handle non-finite values.
Results may differ from a plain program's by a relative error of at most 0.01.
Values may be sent and summed in bfloat16 or wider, within the bound.
A program may use at most 192 MiB of HBM per device.

v0:
```python
import jax
import jax.numpy as jnp
from jax import lax
from jax.sharding import PartitionSpec as P

EXPERTS = 64
TOP = 6
CAP = 15
BETA_ONE = 0.9
BETA_TWO = 0.999
EPSILON = 1e-08
LEARN_RATE = 0.001
WEIGHT_DECAY = 0.1
FIRST_FIX = 1.0 - 0.9**50 * 0.9**50
SECOND_FIX = 1.0 - 0.999**50 * 0.999**50


def gelu_parts(preact):

    def smooth(values):
        return jax.nn.gelu(values, approximate=True)

    result, pullback = jax.vjp(smooth, preact)
    return (result, pullback(jnp.ones_like(preact))[0])


def slot_table(chosen_block):
    chosen = chosen_block.reshape(-1)
    onehot = (chosen[:, None] == jnp.arange(EXPERTS, dtype=jnp.int32)[None, :]).astype(jnp.int32)
    earlier = jnp.cumsum(onehot, axis=0) - onehot
    return (chosen, jnp.sum(earlier * onehot, axis=1))


def adamw_update(weight, gradient, first, second):
    first_new = BETA_ONE * first + (1.0 - BETA_ONE) * gradient
    second_new = BETA_TWO * second + (1.0 - BETA_TWO) * gradient * gradient
    update = first_new / FIRST_FIX / (jnp.sqrt(second_new / SECOND_FIX) + EPSILON)
    current = weight.astype(jnp.float32)
    return (
        (current - LEARN_RATE * (update + WEIGHT_DECAY * current)).astype(jnp.bfloat16),
        first_new,
        second_new,
    )


def expert_pass(inputs, grads_in, w_gate, w_up, w_down):
    gate_projection = jnp.einsum("erd,edf->erf", inputs, w_gate, preferred_element_type=jnp.float32)
    up_projection = jnp.einsum("erd,edf->erf", inputs, w_up, preferred_element_type=jnp.float32)
    sigmoid_gate = jax.nn.sigmoid(gate_projection)
    silu_gate = gate_projection * sigmoid_gate
    inner_activation = (silu_gate * up_projection).astype(jnp.bfloat16)
    out_part = jnp.einsum(
        "erf,efd->erd", inner_activation, w_down, preferred_element_type=jnp.float32
    ).astype(jnp.bfloat16)
    down_weight_gradient = jnp.einsum(
        "erd,efd->erf", grads_in, w_down, preferred_element_type=jnp.float32
    )
    gate_weight_gradient = (
        down_weight_gradient
        * up_projection
        * sigmoid_gate
        * (1.0 + gate_projection * (1.0 - sigmoid_gate))
    ).astype(jnp.bfloat16)
    up_weight_gradient = (down_weight_gradient * silu_gate).astype(jnp.bfloat16)
    input_part = (
        jnp.einsum("erf,edf->erd", gate_weight_gradient, w_gate, preferred_element_type=jnp.float32)
        + jnp.einsum("erf,edf->erd", up_weight_gradient, w_up, preferred_element_type=jnp.float32)
    ).astype(jnp.bfloat16)
    return (out_part, input_part)


def slot_sources(position, flat_weights, total_slots):
    pair_count = position.shape[0]
    owner = (
        jnp.zeros((total_slots,), jnp.int32)
        .at[position]
        .set(jnp.arange(pair_count, dtype=jnp.int32) + 1)
    )
    live = owner > 0
    pair_id = jnp.maximum(owner - 1, 0)
    source_row = pair_id // TOP
    slot_weight = jnp.where(live, flat_weights[pair_id], 0.0)
    return (live, source_row, slot_weight)


def fill_inputs(rows, live, source_row):
    return jnp.where(live[:, None], rows[source_row], jnp.zeros((), rows.dtype))


def fill_grads(grads, slot_weight, source_row):
    return (slot_weight[:, None] * grads[source_row].astype(jnp.float32)).astype(jnp.bfloat16)


def collect_rows(buffer, pair_slots, pair_weights):
    flat = buffer.reshape(-1, buffer.shape[-1])
    total = jnp.zeros((pair_slots.shape[0], flat.shape[1]), jnp.float32)
    for choice_index in range(TOP):
        picked = flat[pair_slots[:, choice_index]].astype(jnp.float32)
        if pair_weights is None:
            total = total + picked
        else:
            total = total + pair_weights[:, choice_index : choice_index + 1] * picked
    return total


def embed_columns(columns, column_start, model_width):
    canvas = jnp.zeros((columns.shape[0], model_width), jnp.float32)
    return lax.dynamic_update_slice_in_dim(canvas, columns.astype(jnp.float32), column_start, 1)


def local(
    features,
    proj_in,
    proj_out,
    expert_gate,
    expert_up,
    expert_down,
    routes,
    gate_weights,
    cotangent,
    first_in,
    second_in,
    first_out,
    second_out,
):
    row_count = features.shape[0]
    model_width = cotangent.shape[1]
    data_parts = lax.axis_size("dp")
    model_parts = lax.axis_size("mp")
    data_place = lax.axis_index("dp")
    model_place = lax.axis_index("mp")
    column_width = model_width // model_parts
    column_start = model_place * column_width
    own_experts = expert_gate.shape[0]
    total_slots = own_experts * data_parts * CAP
    expert_rows = data_parts * CAP
    preact = jnp.dot(
        features,
        lax.all_gather(proj_in, "dp", axis=0, tiled=True),
        preferred_element_type=jnp.float32,
    )
    activated, gelu_slope = gelu_parts(preact)
    hidden = activated.astype(jnp.bfloat16)
    partial_value = jnp.dot(hidden, proj_out, preferred_element_type=jnp.float32)
    chosen, slot_index = slot_table(routes)
    position = chosen * CAP + slot_index
    pair_slots = position.reshape(row_count, TOP)
    live, source_row, slot_weight = slot_sources(position, gate_weights.reshape(-1), total_slots)
    cotangent_cols = lax.dynamic_slice_in_dim(cotangent, column_start, column_width, 1)
    mapped_cols = lax.psum_scatter(partial_value, "mp", scatter_dimension=1, tiled=True).astype(
        jnp.bfloat16
    )
    send_rows = fill_inputs(mapped_cols, live, source_row)
    send_grads = fill_grads(cotangent_cols, slot_weight, source_row)
    send_shape = (data_parts, own_experts, CAP, column_width)
    narrow_rows, narrow_grads = (
        lax.all_to_all(
            send_rows.reshape(send_shape), "dp", split_axis=0, concat_axis=2, tiled=True
        ),
        lax.all_to_all(
            send_grads.reshape(send_shape), "dp", split_axis=0, concat_axis=2, tiled=True
        ),
    )
    recv_rows, recv_grads = (
        lax.all_gather(narrow_rows, "mp", axis=3, tiled=True),
        lax.all_gather(narrow_grads, "mp", axis=3, tiled=True),
    )
    out_part, input_part = expert_pass(
        recv_rows.reshape(own_experts, expert_rows, model_width),
        recv_grads.reshape(own_experts, expert_rows, model_width),
        expert_gate,
        expert_up,
        expert_down,
    )
    back_shape = (1, own_experts, expert_rows, model_width)
    back_out, back_in = (
        lax.all_to_all(out_part.reshape(back_shape), "dp", split_axis=2, concat_axis=0, tiled=True),
        lax.all_to_all(
            input_part.reshape(back_shape), "dp", split_axis=2, concat_axis=0, tiled=True
        ),
    )
    out_terms = collect_rows(back_out, pair_slots, gate_weights) + embed_columns(
        mapped_cols, column_start, model_width
    )
    grad_terms_sum = collect_rows(back_in, pair_slots, None) + embed_columns(
        cotangent_cols, column_start, model_width
    )
    total_out, total_in = lax.psum((out_terms, grad_terms_sum), "mp")
    moe_out = total_out.astype(jnp.bfloat16)
    grad_mapped = total_in.astype(jnp.bfloat16)
    grad_hidden = lax.dot_general(
        grad_mapped, proj_out, (((1,), (1,)), ((), ())), preferred_element_type=jnp.float32
    )
    grad_pre = (grad_hidden * gelu_slope).astype(jnp.bfloat16)
    vis_part = features.shape[1] // data_parts
    width_part = model_width // data_parts
    share_rows = vis_part + width_part
    feature_blocks = features.reshape(row_count, data_parts, vis_part)
    mapped_blocks = grad_mapped.reshape(row_count, data_parts, width_part)
    term_in = jnp.einsum(
        "tnv,th->nvh", feature_blocks, grad_pre, preferred_element_type=jnp.float32
    )
    term_out = jnp.einsum("tnd,th->ndh", mapped_blocks, hidden, preferred_element_type=jnp.float32)
    shares = lax.psum_scatter(
        jnp.concatenate([term_in, term_out], axis=1)
        .reshape(share_rows * lax.axis_size("dp"), hidden.shape[1])
        .astype(jnp.bfloat16),
        "dp",
        scatter_dimension=0,
        tiled=True,
    ).astype(jnp.float32)
    grad_in = shares[:vis_part]
    grad_out = shares[vis_part:].T
    own_out = lax.dynamic_slice_in_dim(proj_out, data_place * width_part, width_part, 1)
    new_in, first_in_new, second_in_new = adamw_update(proj_in, grad_in, first_in, second_in)
    new_out, first_out_new, second_out_new = adamw_update(own_out, grad_out, first_out, second_out)
    return (moe_out, new_in, new_out, first_in_new, second_in_new, first_out_new, second_out_new)


def solution(mesh):
    return jax.shard_map(
        local,
        mesh=mesh,
        in_specs=(
            P("dp", None),
            P("dp", "mp"),
            P("mp", None),
            P("dp", None, "mp"),
            P("dp", None, "mp"),
            P("dp", "mp", None),
            P("dp", None),
            P("dp", None),
            P("dp", None),
            P("dp", "mp"),
            P("dp", "mp"),
            P("mp", "dp"),
            P("mp", "dp"),
        ),
        out_specs=(
            P("dp", None),
            P("dp", "mp"),
            P("mp", "dp"),
            P("dp", "mp"),
            P("dp", "mp"),
            P("mp", "dp"),
            P("mp", "dp"),
        ),
        check_vma=False,
    )
```

profile of v0, /device:TPU:0, one launch (start us, length us, event | category | flops | bytes accessed | tf_op | source)
XLA Modules:
  0.0 924.7 jit_solution(17657232542428289778)
XLA Ops:
  7.9 100.7 %all-gather.4.cloned.1.call-done = bf16[4608,1280]{1,0:T(8,128)(2,1)} async-done(((bf16[288,1280]{1,0:T(8,128)(2,1)}), bf16[4608,1280]{1,0:T(8,128)(2,1)}) %all-gather.4.cloned.1.call-update) | async-done | bytes 11796496 | tf_op jit(solution)/shard_map/all_gather | solution.py:139
  108.6 6.4 fusion.52
  131.4 10.4 %reduce-scatter.3.cloned.1.call-done = f32[128,1280]{1,0:T(8,128)} async-done(((f32[128,2560]{1,0:T(8,128)}), f32[128,1280]{1,0:T(8,128)}) %reduce-scatter.3.cloned.1.call-update) | async-done | bytes 655376 | tf_op jit(solution)/shard_map/reduce_scatter | solution.py:150
  152.8 60.9 %all_to_all.66 = bf16[16,4,15,1280]{3,1,2,0:T(4,128)(2,1)S(1)} all-to-all(bf16[16,4,15,1280]{3,1,2,0:T(4,128)(2,1)S(1)} %copy.63), channel_id=1, replica_groups=mesh['dp'=16,'mp'=2] {'dp'}, dimensions={0} | all-to-all | bytes 4915200 | tf_op jit(solution)/shard_map/all_to_all | solution.py:157
  234.1 45.4 %all-gather.6.cloned.1.call-done = bf16[1,4,240,2560]{3,2,1,0:T(8,128)(2,1)} async-done(((bf16[1,4,240,1280]{3,2,1,0:T(8,128)(2,1)}), bf16[1,4,240,2560]{3,2,1,0:T(8,128)(2,1)}) %all-gather.6.cloned.1.call-update) | async-done | bytes 4915216 | tf_op jit(solution)/shard_map/all_gather | solution.py:165
  279.5 12.7 %fusion.3 = f32[4,240,768]{2,1,0:T(8,128)} fusion(bf16[4,2560,768]{2,1,0:T(8,128)(2,1)} %param.17, bf16[1,4,240,2560]{3,2,1,0:T(8,128)(2,1)} %all-gather.6.cloned.1.call-done), kind=kOutput, calls=%fused_computation.25 | convolution fusion | flops 3774873600 | bytes 23592960 | tf_op jit(solution)/shard_map/erd,edf->erf/dot_general | solution.py:48
  292.3 7.6 fusion.5
  299.8 13.6 %fusion.7 = bf16[1,4,240,2560]{3,2,1,0:T(8,128)(2,1)} fusion(bf16[4,768,2560]{2,1,0:T(8,128)(2,1)} %param.18, f32[4,240,768]{2,1,0:T(8,128)} %fusion.3, f32[4,240,768]{2,1,0:T(8,128)S(1)} %fusion.5), kind=kOutput, calls=%fused_computation.29 | convolution fusion | flops 3781754880 | bytes 26542080 | tf_op jit(solution)/shard_map/erf,efd->erd/dot_general | solution.py:52
  313.5 8.4 copy.65
  321.9 5.7 all-to-all-start.1
  329.8 65.3 %all-gather.8.cloned.1.call-done = bf16[1,4,240,2560]{3,2,1,0:T(8,128)(2,1)} async-done(((bf16[1,4,240,1280]{3,2,1,0:T(8,128)(2,1)}), bf16[1,4,240,2560]{3,2,1,0:T(8,128)(2,1)}) %all-gather.8.cloned.1.call-update) | async-done | bytes 4915216 | tf_op jit(solution)/shard_map/all_gather | solution.py:166
  395.2 12.8 %fusion.1 = f32[4,240,768]{2,1,0:T(8,128)} fusion(bf16[4,768,2560]{2,1,0:T(8,128)(2,1)} %param.18, bf16[1,4,240,2560]{3,2,1,0:T(8,128)(2,1)} %all-gather.8.cloned.1.call-done), kind=kOutput, calls=%fused_computation.23 | convolution fusion | flops 3774873600 | bytes 23592960 | tf_op jit(solution)/shard_map/erd,efd->erf/dot_general | solution.py:55
  408.0 13.0 %fusion.16 = f32[4,240,2560]{2,1,0:T(8,128)} fusion(bf16[4,2560,768]{2,1,0:T(8,128)(2,1)} %param.16, f32[4,240,768]{2,1,0:T(8,128)} %copy-done.2, f32[4,240,768]{2,1,0:T(8,128)} %fusion.1, f32[4,240,768]{2,1,0:T(8,128)} %fusion.3), kind=kOutput, calls=%fused_computation.47 | convolution fusion | flops 3782246400 | bytes 34406400 | tf_op jit(solution)/shard_map/erf,edf->erd/dot_general | solution.py:66
  420.9 14.6 %fusion.8 = bf16[1,4,240,2560]{3,2,1,0:T(8,128)(2,1)} fusion(f32[4,240,2560]{2,1,0:T(8,128)} %fusion.16, bf16[4,2560,768]{2,1,0:T(8,128)(2,1)} %param.17, f32[4,240,768]{2,1,0:T(8,128)} %fusion.1, f32[4,240,768]{2,1,0:T(8,128)} %copy-done.2), kind=kOutput, calls=%fused_computation.30 | convolution fusion | flops 3784212480 | bytes 36372480 | tf_op jit(solution)/shard_map/erf,edf->erd/dot_general | solution.py:67
  435.5 8.5 copy.70
  444.0 5.8 all-to-all-start.3
  451.6 5.9 copy.66
  457.5 7.6 reshape.114
  474.4 65.5 %all-to-all-done.3 = bf16[1,4,240,2560]{3,1,0,2:T(4,128)(2,1)} async-done(((bf16[1,4,240,2560]{3,1,0,2:T(4,128)(2,1)}), bf16[1,4,240,2560]{3,1,0,2:T(4,128)(2,1)}, u32[]{:S(2)}, u32[]{:S(2)}) %all-to-all-start.3) | async-done | bytes 4915232 | tf_op jit(solution)/shard_map/all_to_all | solution.py:178
  539.9 6.0 copy.71
  545.9 7.8 reshape.118
  553.7 5.5 gather_fusion.14
  559.2 5.5 gather_fusion.13
  564.6 5.5 gather_fusion.4
  575.6 5.5 gather_fusion.3
  581.1 5.5 gather_fusion.11
  586.6 5.7 gather_fusion.2
  592.3 5.5 gather_fusion.10
  603.3 5.5 gather_fusion.9
  613.1 66.1 %all-reduce.2 = (bf16[128,2560]{1,0:T(8,128)(2,1)}, bf16[128,2560]{1,0:T(8,128)(2,1)}) all-reduce(f32[128,2560]{1,0:T(8,128)S(1)} %add_dynamic-update-slice_fusion.1, f32[128,2560]{1,0:T(8,128)S(1)} %add_dynamic-update-slice_fusion), channel_id=1, replica_groups=mesh['dp'=16,'mp'=2] {'mp'}, use_global_device_ids=true, to_apply=%region_5.6 | all-reduce | flops 655360 | bytes 3932160 | tf_op jit(solution)/shard_map/psum | solution.py:188
  694.2 10.9 %pad_maximum_fusion = bf16[16,448,1280]{2,1,0:T(8,128)(2,1)} fusion(bf16[16,160,1280]{2,1,0:T(8,128)(2,1)} %convolution_convert_fusion.1, bf16[16,288,1280]{2,1,0:T(8,128)(2,1)S(1)} %fusion), kind=kLoop, calls=%fused_computation.16 | loop fusion | flops 36700160 | bytes 36700160 | tf_op jit(solution)/shard_map/concatenate | solution.py:205
  707.1 204.6 %reduce-scatter.5.cloned.1.call-done = bf16[448,1280]{1,0:T(8,128)(2,1)} async-done(((bf16[7168,1280]{1,0:T(8,128)(2,1)}), bf16[448,1280]{1,0:T(8,128)(2,1)}) %reduce-scatter.5.cloned.1.call-update) | async-done | bytes 1146896 | tf_op jit(solution)/shard_map/reduce_scatter | solution.py:204
  (112 shorter events, 99.5 us)
Async XLA Ops:
  7.2 101.4 %all-gather.4.cloned.1.call-start = ((), (), s32[]{:S(2)}) async-start(), calls=%async_computation.6 | async-start | bytes 12533760 | tf_op jit(solution)/shard_map/all_gather | solution.py:139
  7.9 133.9 %reduce-scatter.3.cloned.1.call-start = ((), (), s32[]{:S(2)}) async-start(), calls=%async_computation.7 | async-start | bytes 1966080 | tf_op jit(solution)/shard_map/reduce_scatter | solution.py:150
  115.0 5.1 copy-start.18
  115.0 8.1 copy-start.17
  120.1 159.4 %all-gather.6.cloned.1.call-start = ((), (), s32[]{:S(2)}) async-start(), calls=%async_computation.8 | async-start | bytes 7372800 | tf_op jit(solution)/shard_map/all_gather | solution.py:165
  213.7 1.8 copy-start.15
  229.2 92.7 %all-to-all-start.2 = ((bf16[16,4,15,1280]{3,1,2,0:T(4,128)(2,1)}), bf16[16,4,15,1280]{3,1,2,0:T(4,128)(2,1)S(1)}, u32[]{:S(2)}, u32[]{:S(2)}) async-start(bf16[16,4,15,1280]{3,1,2,0:T(4,128)(2,1)} %copy.68), calls=%async_computation.3 | async-start | bytes 4915200 | tf_op jit(solution)/shard_map/all_to_all | solution.py:160
  279.5 12.8 %copy-start.19 = (bf16[1,4,240,2560]{3,2,1,0:T(8,128)(2,1)S(1)}, bf16[1,4,240,2560]{3,2,1,0:T(8,128)(2,1)}, u32[]{:S(2)}) copy-start(bf16[1,4,240,2560]{3,2,1,0:T(8,128)(2,1)} %all-gather.6.cloned.1.call-done) | copy-start | bytes 14745604
  299.8 13.7 %copy-start.2 = (f32[4,240,768]{2,1,0:T(8,128)}, f32[4,240,768]{2,1,0:T(8,128)S(1)}, u32[]{:S(2)}) copy-start(f32[4,240,768]{2,1,0:T(8,128)S(1)} %fusion.5) | copy-start | bytes 8847364
  321.9 122.1 %all-to-all-start.1 = ((bf16[1,4,240,2560]{3,1,0,2:T(4,128)(2,1)}), bf16[1,4,240,2560]{3,1,0,2:T(4,128)(2,1)}, u32[]{:S(2)}, u32[]{:S(2)}) async-start(bf16[1,4,240,2560]{3,1,0,2:T(4,128)(2,1)} %copy.65), calls=%async_computation.2 | async-start | bytes 9830400 | tf_op jit(solution)/shard_map/all_to_all | solution.py:177
  327.6 67.6 %all-gather.8.cloned.1.call-start = ((), (), s32[]{:S(2)}) async-start(), calls=%async_computation.9 | async-start | bytes 7372800 | tf_op jit(solution)/shard_map/all_gather | solution.py:166
  444.0 5.9 copy-start
  444.0 95.9 %all-to-all-start.3 = ((bf16[1,4,240,2560]{3,1,0,2:T(4,128)(2,1)}), bf16[1,4,240,2560]{3,1,0,2:T(4,128)(2,1)}, u32[]{:S(2)}, u32[]{:S(2)}) async-start(bf16[1,4,240,2560]{3,1,0,2:T(4,128)(2,1)} %copy.70), calls=%async_computation.4 | async-start | bytes 9830400 | tf_op jit(solution)/shard_map/all_to_all | solution.py:178
  449.8 461.9 %reduce-scatter.5.cloned.1.call-start = ((), (), s32[]{:S(2)}) async-start(), calls=%async_computation.10 | async-start | bytes 19496960 | tf_op jit(solution)/shard_map/reduce_scatter | solution.py:204
  608.8 2.7 copy-start.10
  608.8 2.8 copy-start.4
  608.8 2.9 copy-start.5
  608.8 2.9 copy-start.6
  608.8 2.9 copy-start.7
  608.8 2.9 copy-start.8
  608.8 3.0 copy-start.9
  611.9 1.1 copy-start.16
  686.0 4.6 copy-start.1
  705.2 208.1 %copy-start.3 = (bf16[288,1280]{1,0:T(8,128)(2,1)S(1)}, bf16[288,1280]{1,0:T(8,128)(2,1)}, u32[]{:S(2)}) copy-start(bf16[288,1280]{1,0:T(8,128)(2,1)} %param.14) | copy-start | bytes 2211844
  705.2 208.1 %copy-start.11 = (f32[288,1280]{1,0:T(8,128)S(1)}, f32[288,1280]{1,0:T(8,128)}, u32[]{:S(2)}) copy-start(f32[288,1280]{1,0:T(8,128)} %param.22) | copy-start | bytes 4423684
  911.7 1.7 copy-start.12
  913.4 2.6 copy-start.13
  913.4 2.6 copy-start.14
Sparse Core Ops, SparseCore 0:
  10.3 98.3 all-gather.3
  120.2 21.5 reduce-scatter.2
  215.7 63.7 all-gather.5
  329.9 65.1 all-gather.7
  705.3 206.3 reduce-scatter.4
where the time goes:
time: 934 us; the launch traced here: 925 us
  waiting for transfers between devices  493 us (53%)
  local copies, waits for them, and re-layouts  147 us (16%)
  blocking collectives  127 us (14%)
  matrix products  99.3 us (11%)
  other arithmetic  27.3 us (3%)
  starting transfers between devices  17 us (2%)
  between operations  14.7 us (2%)
    reduce_scatter x1, waiting for transfers between devices, local(): lax.psum_scatter(jnp.concatenate([term_in, term_out], axis=1).reshape(sha...  205 us
    all_gather x1, waiting for transfers between devices, local(): lax.all_gather(proj_in, 'dp', axis=0, tiled=True)  101 us
    psum x1, blocking collectives, local(): total_out, total_in = lax.psum((out_terms, grad_terms_sum), 'mp')  66.1 us
    all_to_all x1, waiting for transfers between devices, local(): lax.all_to_all(input_part.reshape(back_shape), 'dp', split_axis=2, concat...  65.5 us
    all_gather x1, waiting for transfers between devices, local(): lax.all_gather(narrow_grads, 'mp', axis=3, tiled=True)  65.3 us
    gather x12, local copies, waits for them, and re-layouts, collect_rows(): picked = flat[pair_slots[:, choice_index]].astype(jnp.float32)  64.4 us
    all_to_all x1, blocking collectives, local(): lax.all_to_all(send_rows.reshape(send_shape), 'dp', split_axis=0, concat_...  60.9 us
    all_gather x1, waiting for transfers between devices, local(): lax.all_gather(narrow_rows, 'mp', axis=3, tiled=True)  45.4 us
  transfers between devices with their start and end apart: 8, of which 6 were waited for; matrix products, arithmetic and copies ran while one was open for 16% of the time, Pallas kernels for 0%

commit v1 on v0

--- a/solution.py
+++ b/solution.py
@@ -13,6 +13,12 @@
 WEIGHT_DECAY = 0.1
 FIRST_FIX = 1.0 - 0.9**50 * 0.9**50
 SECOND_FIX = 1.0 - 0.999**50 * 0.999**50
+
+
+def stack_and_merge(shard, mesh_axis, dim):
+    parts = lax.all_gather(shard, mesh_axis, axis=0, tiled=False)
+    whole = jnp.concatenate(parts, axis=dim)
+    return whole
 
 
 def gelu_parts(preact):
@@ -163,7 +169,7 @@
     )
     recv_rows, recv_grads = (
         lax.all_gather(narrow_rows, "mp", axis=3, tiled=True),
-        lax.all_gather(narrow_grads, "mp", axis=3, tiled=True),
+        stack_and_merge(narrow_grads, "mp", 3),
     )
     out_part, input_part = expert_pass(
         recv_rows.reshape(own_experts, expert_rows, model_width),

time: 934 us -> 966 us (1.034)
  local copies, waits for them, and re-layouts: 147 us -> 168 us
    another operation x0 -> x1, local copies, waits for them, and re-layouts: none -> 11.6 us  [local(): recv_grads.reshape(own_experts, expert_rows, model_width)]
    reshape x0 -> x1, local copies, waits for them, and re-layouts: none -> 9.68 us  [stack_and_merge(): whole = jnp.concatenate(parts, axis=dim)]
  transfers between devices with their start and end apart: 8 -> 8, of which waited for: 6 -> 6; matrix products, arithmetic and copies ran while one was open for 16% -> 17% of each run, Pallas kernels for 0% -> 0%
where the time goes in v1:
time: 966 us; the launch traced here: 956 us
  waiting for transfers between devices  493 us (51%)
  local copies, waits for them, and re-layouts  168 us (17%)
  blocking collectives  127 us (13%)
  matrix products  99.7 us (10%)
  other arithmetic  27.3 us (3%)
  starting transfers between devices  26.5 us (3%)
  between operations  14.7 us (2%)
    reduce_scatter x1, waiting for transfers between devices, local(): lax.psum_scatter(jnp.concatenate([term_in, term_out], axis=1).reshape(sha...  205 us
    all_gather x1, waiting for transfers between devices, local(): lax.all_gather(proj_in, 'dp', axis=0, tiled=True)  101 us
    psum x1, blocking collectives, local(): total_out, total_in = lax.psum((out_terms, grad_terms_sum), 'mp')  66.1 us
    all_to_all x1, waiting for transfers between devices, local(): lax.all_to_all(input_part.reshape(back_shape), 'dp', split_axis=2, concat...  65.5 us
    all_gather x1, waiting for transfers between devices, stack_and_merge(): parts = lax.all_gather(shard, mesh_axis, axis=0, tiled=False)  65.3 us
    gather x12, local copies, waits for them, and re-layouts, collect_rows(): picked = flat[pair_slots[:, choice_index]].astype(jnp.float32)  64.4 us
    all_to_all x1, blocking collectives, local(): lax.all_to_all(send_rows.reshape(send_shape), 'dp', split_axis=0, concat_...  61 us
    all_gather x1, waiting for transfers between devices, local(): lax.all_gather(narrow_rows, 'mp', axis=3, tiled=True)  45.3 us
  transfers between devices with their start and end apart: 8, of which 6 were waited for; matrix products, arithmetic and copies ran while one was open for 17% of the time, Pallas kernels for 0%

profile of v1, /device:TPU:0, one launch (start us, length us, event | category | flops | bytes accessed | tf_op | source)
XLA Modules:
  0.0 955.8 jit_solution(15266181214440915968)
XLA Ops:
  7.9 100.7 %all-gather.4.cloned.1.call-done = bf16[4608,1280]{1,0:T(8,128)(2,1)} async-done(((bf16[288,1280]{1,0:T(8,128)(2,1)}), bf16[4608,1280]{1,0:T(8,128)(2,1)}) %all-gather.4.cloned.1.call-update) | async-done | bytes 11796496 | tf_op jit(solution)/shard_map/all_gather | solution.py:145
  108.6 6.4 fusion.50
  131.4 10.4 %reduce-scatter.3.cloned.1.call-done = f32[128,1280]{1,0:T(8,128)} async-done(((f32[128,2560]{1,0:T(8,128)}), f32[128,1280]{1,0:T(8,128)}) %reduce-scatter.3.cloned.1.call-update) | async-done | bytes 655376 | tf_op jit(solution)/shard_map/reduce_scatter | solution.py:156
  152.8 61.0 %all_to_all.63 = bf16[16,4,15,1280]{3,1,2,0:T(4,128)(2,1)S(1)} all-to-all(bf16[16,4,15,1280]{3,1,2,0:T(4,128)(2,1)S(1)} %copy.63), channel_id=1, replica_groups=mesh['dp'=16,'mp'=2] {'dp'}, dimensions={0} | all-to-all | bytes 4915200 | tf_op jit(solution)/shard_map/all_to_all | solution.py:163
  234.2 45.3 %all-gather.6.cloned.1.call-done = bf16[1,4,240,2560]{3,2,1,0:T(8,128)(2,1)} async-done(((bf16[1,4,240,1280]{3,2,1,0:T(8,128)(2,1)}), bf16[1,4,240,2560]{3,2,1,0:T(8,128)(2,1)}) %all-gather.6.cloned.1.call-update) | async-done | bytes 4915216 | tf_op jit(solution)/shard_map/all_gather | solution.py:171
  279.5 12.7 %fusion.1 = f32[4,240,768]{2,1,0:T(8,128)} fusion(bf16[4,2560,768]{2,1,0:T(8,128)(2,1)} %param.17, bf16[1,4,240,2560]{3,2,1,0:T(8,128)(2,1)} %all-gather.6.cloned.1.call-done), kind=kOutput, calls=%fused_computation.23 | convolution fusion | flops 3774873600 | bytes 23592960 | tf_op jit(solution)/shard_map/erd,edf->erf/dot_general | solution.py:54
  292.3 7.6 fusion.3
  299.8 13.6 %fusion.5 = bf16[1,4,240,2560]{3,2,1,0:T(8,128)(2,1)} fusion(bf16[4,768,2560]{2,1,0:T(8,128)(2,1)} %param.18, f32[4,240,768]{2,1,0:T(8,128)} %fusion.1, f32[4,240,768]{2,1,0:T(8,128)S(1)} %fusion.3), kind=kOutput, calls=%fused_computation.27 | convolution fusion | flops 3781754880 | bytes 26542080 | tf_op jit(solution)/shard_map/erf,efd->erd/dot_general | solution.py:58
  313.5 8.4 copy.65
  321.9 5.7 all-to-all-start.1
  327.6 9.9 %all-gather.8.cloned.1.call-start = ((), (), s32[]{:S(2)}) async-start(), calls=%async_computation.9 | async-start | bytes 7372800 | tf_op jit(solution)/shard_map/all_gather | solution.py:19
  339.2 65.3 %all-gather.8.cloned.1.call-done = bf16[2,1,4,240,1280]{4,3,2,1,0:T(8,128)(2,1)} async-done(((bf16[1,1,4,240,1280]{4,3,2,1,0:T(8,128)(2,1)}), bf16[2,1,4,240,1280]{4,3,2,1,0:T(8,128)(2,1)}) %all-gather.8.cloned.1.call-update) | async-done | bytes 4915216 | tf_op jit(solution)/shard_map/all_gather | solution.py:19
  404.6 9.7 %copy.70 = bf16[1,4,240,2,1280]{4,3,2,1,0:T(2,128)(2,1)} copy(bf16[1,4,240,2,1280]{4,2,1,0,3:T(8,128)(2,1)} %bitcast.98) | data formatting | bytes 9830400 | tf_op jit(solution)/shard_map/reshape | solution.py:20
  414.3 11.6 %reshape_reshape.3 = bf16[4,240,2560]{2,1,0:T(8,128)(2,1)} reshape(bf16[1,4,240,2,1280]{4,3,2,1,0:T(2,128)(2,1)} %copy.70) | data formatting | bytes 9830400 | tf_op jit(solution)/shard_map/reshape;reshape | solution.py:176
  425.9 12.8 %fusion.51 = f32[4,240,768]{2,1,0:T(8,128)} fusion(bf16[4,240,2560]{2,1,0:T(8,128)(2,1)} %reshape_reshape.3, bf16[4,768,2560]{2,1,0:T(8,128)(2,1)} %param.18), kind=kOutput, calls=%fused_computation.128 | convolution fusion | flops 3774873600 | bytes 23592960 | tf_op jit(solution)/shard_map/erd,efd->erf/dot_general | solution.py:61
  438.7 13.0 %fusion.14 = f32[4,240,2560]{2,1,0:T(8,128)} fusion(bf16[4,2560,768]{2,1,0:T(8,128)(2,1)} %param.16, f32[4,240,768]{2,1,0:T(8,128)} %copy-done.2, f32[4,240,768]{2,1,0:T(8,128)} %fusion.51, f32[4,240,768]{2,1,0:T(8,128)} %fusion.1), kind=kOutput, calls=%fused_computation.45 | convolution fusion | flops 3782246400 | bytes 34406400 | tf_op jit(solution)/shard_map/erf,edf->erd/dot_general | solution.py:72
  451.6 15.0 %fusion.6 = bf16[1,4,240,2560]{3,2,1,0:T(8,128)(2,1)} fusion(f32[4,240,2560]{2,1,0:T(8,128)} %fusion.14, bf16[4,2560,768]{2,1,0:T(8,128)(2,1)} %param.17, f32[4,240,768]{2,1,0:T(8,128)} %fusion.51, f32[4,240,768]{2,1,0:T(8,128)} %copy-done.2), kind=kOutput, calls=%fused_computation.28 | convolution fusion | flops 3784212480 | bytes 36372480 | tf_op jit(solution)/shard_map/erf,edf->erd/dot_general | solution.py:73
  466.6 8.5 copy.71
  475.1 5.8 all-to-all-start.3
  482.7 5.9 copy.66
  488.6 7.6 reshape.115
  505.5 65.5 %all-to-all-done.3 = bf16[1,4,240,2560]{3,1,0,2:T(4,128)(2,1)} async-done(((bf16[1,4,240,2560]{3,1,0,2:T(4,128)(2,1)}), bf16[1,4,240,2560]{3,1,0,2:T(4,128)(2,1)}, u32[]{:S(2)}, u32[]{:S(2)}) %all-to-all-start.3) | async-done | bytes 4915232 | tf_op jit(solution)/shard_map/all_to_all | solution.py:184
  571.0 6.0 copy.72
  577.0 7.8 reshape.119
  590.3 5.5 gather_fusion.13
  612.2 5.5 gather_fusion.11
  617.7 5.7 gather_fusion.2
  623.4 5.5 gather_fusion.10
  634.4 5.5 gather_fusion.9
  644.2 66.1 %all-reduce.2 = (bf16[128,2560]{1,0:T(8,128)(2,1)}, bf16[128,2560]{1,0:T(8,128)(2,1)}) all-reduce(f32[128,2560]{1,0:T(8,128)S(1)} %add_dynamic-update-slice_fusion.1, f32[128,2560]{1,0:T(8,128)S(1)} %add_dynamic-update-slice_fusion), channel_id=1, replica_groups=mesh['dp'=16,'mp'=2] {'mp'}, use_global_device_ids=true, to_apply=%region_5.6 | all-reduce | flops 655360 | bytes 3932160 | tf_op jit(solution)/shard_map/psum | solution.py:194
  725.3 10.9 %pad_maximum_fusion = bf16[16,448,1280]{2,1,0:T(8,128)(2,1)} fusion(bf16[16,160,1280]{2,1,0:T(8,128)(2,1)} %convolution_convert_fusion.1, bf16[16,288,1280]{2,1,0:T(8,128)(2,1)S(1)} %fusion), kind=kLoop, calls=%fused_computation.16 | loop fusion | flops 36700160 | bytes 36700160 | tf_op jit(solution)/shard_map/concatenate | solution.py:211
  738.2 204.6 %reduce-scatter.5.cloned.1.call-done = bf16[448,1280]{1,0:T(8,128)(2,1)} async-done(((bf16[7168,1280]{1,0:T(8,128)(2,1)}), bf16[448,1280]{1,0:T(8,128)(2,1)}) %reduce-scatter.5.cloned.1.call-update) | async-done | bytes 1146896 | tf_op jit(solution)/shard_map/reduce_scatter | solution.py:210
  (114 shorter events, 115.6 us)
Async XLA Ops:
  7.2 101.4 %all-gather.4.cloned.1.call-start = ((), (), s32[]{:S(2)}) async-start(), calls=%async_computation.6 | async-start | bytes 12533760 | tf_op jit(solution)/shard_map/all_gather | solution.py:145
  7.9 133.9 %reduce-scatter.3.cloned.1.call-start = ((), (), s32[]{:S(2)}) async-start(), calls=%async_computation.7 | async-start | bytes 1966080 | tf_op jit(solution)/shard_map/reduce_scatter | solution.py:156
  115.0 5.1 copy-start.18
  115.0 8.1 copy-start.17
  120.1 159.4 %all-gather.6.cloned.1.call-start = ((), (), s32[]{:S(2)}) async-start(), calls=%async_computation.8 | async-start | bytes 7372800 | tf_op jit(solution)/shard_map/all_gather | solution.py:171
  213.8 1.8 copy-start.15
  229.2 92.7 %all-to-all-start.2 = ((bf16[16,4,15,1280]{3,1,2,0:T(4,128)(2,1)}), bf16[16,4,15,1280]{3,1,2,0:T(4,128)(2,1)S(1)}, u32[]{:S(2)}, u32[]{:S(2)}) async-start(bf16[16,4,15,1280]{3,1,2,0:T(4,128)(2,1)} %copy.68), calls=%async_computation.3 | async-start | bytes 4915200 | tf_op jit(solution)/shard_map/all_to_all | solution.py:166
  279.5 12.8 %copy-start.19 = (bf16[1,4,240,2560]{3,2,1,0:T(8,128)(2,1)S(1)}, bf16[1,4,240,2560]{3,2,1,0:T(8,128)(2,1)}, u32[]{:S(2)}) copy-start(bf16[1,4,240,2560]{3,2,1,0:T(8,128)(2,1)} %all-gather.6.cloned.1.call-done) | copy-start | bytes 14745604
  299.8 13.7 %copy-start.2 = (f32[4,240,768]{2,1,0:T(8,128)}, f32[4,240,768]{2,1,0:T(8,128)S(1)}, u32[]{:S(2)}) copy-start(f32[4,240,768]{2,1,0:T(8,128)S(1)} %fusion.3) | copy-start | bytes 8847364
  321.9 153.2 %all-to-all-start.1 = ((bf16[1,4,240,2560]{3,1,0,2:T(4,128)(2,1)}), bf16[1,4,240,2560]{3,1,0,2:T(4,128)(2,1)}, u32[]{:S(2)}, u32[]{:S(2)}) async-start(bf16[1,4,240,2560]{3,1,0,2:T(4,128)(2,1)} %copy.65), calls=%async_computation.2 | async-start | bytes 9830400 | tf_op jit(solution)/shard_map/all_to_all | solution.py:183
  327.6 77.0 %all-gather.8.cloned.1.call-start = ((), (), s32[]{:S(2)}) async-start(), calls=%async_computation.9 | async-start | bytes 7372800 | tf_op jit(solution)/shard_map/all_gather | solution.py:19
  475.1 5.9 copy-start
  475.1 95.9 %all-to-all-start.3 = ((bf16[1,4,240,2560]{3,1,0,2:T(4,128)(2,1)}), bf16[1,4,240,2560]{3,1,0,2:T(4,128)(2,1)}, u32[]{:S(2)}, u32[]{:S(2)}) async-start(bf16[1,4,240,2560]{3,1,0,2:T(4,128)(2,1)} %copy.71), calls=%async_computation.4 | async-start | bytes 9830400 | tf_op jit(solution)/shard_map/all_to_all | solution.py:184
  480.9 461.9 %reduce-scatter.5.cloned.1.call-start = ((), (), s32[]{:S(2)}) async-start(), calls=%async_computation.10 | async-start | bytes 19496960 | tf_op jit(solution)/shard_map/reduce_scatter | solution.py:210
  639.9 2.7 copy-start.10
  639.9 2.8 copy-start.4
  639.9 2.9 copy-start.5
  639.9 2.9 copy-start.6
  639.9 2.9 copy-start.7
  639.9 2.9 copy-start.8
  639.9 3.0 copy-start.9
  643.0 1.1 copy-start.16
  717.1 4.6 copy-start.1
  736.3 208.1 %copy-start.3 = (bf16[288,1280]{1,0:T(8,128)(2,1)S(1)}, bf16[288,1280]{1,0:T(8,128)(2,1)}, u32[]{:S(2)}) copy-start(bf16[288,1280]{1,0:T(8,128)(2,1)} %param.14) | copy-start | bytes 2211844
  736.3 208.1 %copy-start.11 = (f32[288,1280]{1,0:T(8,128)S(1)}, f32[288,1280]{1,0:T(8,128)}, u32[]{:S(2)}) copy-start(f32[288,1280]{1,0:T(8,128)} %param.22) | copy-start | bytes 4423684
  942.8 1.7 copy-start.12
  944.5 2.6 copy-start.13
  944.5 2.6 copy-start.14
Sparse Core Ops, SparseCore 0:
  10.3 98.3 all-gather.3
  120.2 21.5 reduce-scatter.2
  215.7 63.7 all-gather.5
  339.4 65.1 all-gather.7
  736.4 206.3 reduce-scatter.4
